TPU v7x, 32 devices: a whole 2x2x4 slice. The times are simulated.
32 devices in a mesh: row: 8 (over y, x, core), col: 4 (over z).
Axes of the slice: x: 2, y: 2, z: 4, core: 2. Of those that a mesh axis runs over, the one named last changes fastest.
Arguments:
- features: bfloat16 [512, 128, 128], P('row', 'col'), may hold values from -6 to 6
- cotangent: bfloat16 [512, 128, 128], P('row', 'col'), may hold values from -6 to 6
- kernels: bfloat16 [2, 9, 128, 128], replicated, may hold values from -0.1875 to 0.1875
- momentum: float32 [2, 147456], replicated, may hold values from -6 to 6
- mlp_in_weight: float32 [32, 3], replicated, may hold values from -3.5 to 3.5
- mlp_in_bias: float32 [32], replicated, may hold values from -3 to 3
- mlp_out_weight: float32 [2, 32], replicated, may hold values from -1 to 1
- mlp_out_bias: float32 [2], replicated, may hold values from -3 to 3
Outputs:
- update: float32 [2, 147456], replicated
- momentum_out: float32 [2, 147456], replicated
All inputs are finite; a program needn't handle non-finite values.
Results may differ from a plain program's by a relative error of at most 0.0014.
Values may be sent and summed in bfloat16 or wider, within the bound.
A program may use at most 64 MiB of HBM per device.

v0:
```python
import math

import jax
import jax.numpy as jnp
from jax import lax
from jax.sharding import PartitionSpec as P


def padded_2(cells, sides, width):
    for axis, dim in sides:
        count = lax.axis_size(axis)
        head = lax.slice_in_dim(cells, 0, width, axis=dim)
        tail = lax.slice_in_dim(cells, cells.shape[dim] - width, cells.shape[dim], axis=dim)
        cells = jnp.concatenate(
            [
                lax.ppermute(tail, axis, [(i, (i + 1) % count) for i in range(count)]),
                cells,
                lax.ppermute(head, axis, [((i + 1) % count, i) for i in range(count)]),
            ],
            axis=dim,
        )
    return cells


def convolve(padded, kernel, tile_rows, tile_cols):
    channels = padded.shape[-1]
    summed = jnp.zeros((tile_rows * tile_cols, kernel.shape[-1]), jnp.float32)
    for tap_row in range(3):
        for tap_col in range(3):
            window = padded[tap_row : tap_row + tile_rows, tap_col : tap_col + tile_cols].reshape(
                tile_rows * tile_cols, channels
            )
            summed = summed + jnp.dot(
                window, kernel[3 * tap_row + tap_col], preferred_element_type=jnp.float32
            )
    return summed.reshape(tile_rows, tile_cols, -1)


def kernel_grad(padded, cotangent, tile_rows, tile_cols):
    channels = padded.shape[-1]
    flat_cot = cotangent.reshape(tile_rows * tile_cols, -1)
    taps = []
    for tap_row in range(3):
        for tap_col in range(3):
            window = padded[tap_row : tap_row + tile_rows, tap_col : tap_col + tile_cols].reshape(
                tile_rows * tile_cols, channels
            )
            taps.append(
                lax.dot_general(
                    window, flat_cot, (((0,), (0,)), ((), ())), preferred_element_type=jnp.float32
                )
            )
    return jnp.stack(taps)


def transpose_conv(cot_pad, kernel, tile_rows, tile_cols):
    channels = cot_pad.shape[-1]
    summed = jnp.zeros((tile_rows * tile_cols, kernel.shape[-2]), jnp.float32)
    for tap_row in range(3):
        for tap_col in range(3):
            window = cot_pad[
                2 - tap_row : 2 - tap_row + tile_rows, 2 - tap_col : 2 - tap_col + tile_cols
            ].reshape(tile_rows * tile_cols, channels)
            summed = summed + lax.dot_general(
                window,
                kernel[3 * tap_row + tap_col],
                (((1,), (1,)), ((), ())),
                preferred_element_type=jnp.float32,
            )
    return summed.reshape(tile_rows, tile_cols, -1)


def learned_step(grads, squares, momentum, weights, w_in, b_in, w_out, b_out, gain, count):
    norm_scale = 1.0 / jnp.sqrt(squares / count + 1e-06)
    g_hat = grads * norm_scale[:, None]
    momentum_new = 0.9 * momentum + 0.1 * g_hat
    scaled = weights.astype(jnp.float32) * gain
    pre_units = (
        w_in[:, 0][:, None, None] * g_hat[None] + w_in[:, 1][:, None, None] * momentum_new[None]
    )
    pre_units = pre_units + w_in[:, 2][:, None, None] * scaled[None] + b_in[:, None, None]
    units = jax.nn.silu(pre_units)
    mlp_result = (
        jnp.einsum("kh,hlp->klp", w_out, units, precision=lax.Precision.HIGHEST)
        + b_out[:, None, None]
    )
    update = mlp_result[0] * jnp.exp(jnp.tanh(mlp_result[1]))
    return (update, momentum_new)


def on_device(
    features, cotangent, kernels, momentum, mlp_in_weight, mlp_in_bias, mlp_out_weight, mlp_out_bias
):
    tile_rows, tile_cols, channels = features.shape
    param_count = 9 * channels * channels
    image_pad = padded_2(features, (("row", 0), ("col", 1)), 1)
    pre_act = convolve(image_pad, kernels[0], tile_rows, tile_cols)
    hidden = jax.nn.silu(pre_act).astype(jnp.bfloat16)
    hidden_pad = padded_2(hidden, (("row", 0), ("col", 1)), 1)
    cot_pad = padded_2(cotangent, (("row", 0), ("col", 1)), 1)
    grad_two = kernel_grad(hidden_pad, cotangent, tile_rows, tile_cols)
    back_grad = transpose_conv(cot_pad, kernels[1], tile_rows, tile_cols)
    sigma_val = jax.nn.sigmoid(pre_act)
    pre_grad = (back_grad * sigma_val * (1.0 + pre_act * (1.0 - sigma_val))).astype(jnp.bfloat16)
    grad_one = kernel_grad(image_pad, pre_grad, tile_rows, tile_cols)
    local_grads = jnp.stack([grad_one.reshape(-1), grad_two.reshape(-1)])
    weights = kernels.reshape(2, param_count)
    gain = math.sqrt(9.0 * channels)
    grads = lax.psum(local_grads, ("row", "col"))
    squares = jnp.sum(grads * grads, axis=1)
    update, momentum_out = learned_step(
        grads,
        squares,
        momentum,
        weights,
        mlp_in_weight,
        mlp_in_bias,
        mlp_out_weight,
        mlp_out_bias,
        gain,
        float(param_count),
    )
    return (update, momentum_out)


def solution(mesh):
    placed = (P("row", "col", None), P("row", "col", None), P(), P(), P(), P(), P(), P())
    return jax.shard_map(
        on_device, mesh=mesh, in_specs=placed, out_specs=(P(), P()), check_vma=False
    )
```

profile of v0, /device:TPU:1, one launch (start us, length us, event | category | flops | bytes accessed | tf_op | source)
XLA Modules:
  0.0 236.7 jit_solution(3576847353787842551)
XLA Ops:
  7.2 1.3 copy.30
  8.6 2.6 %collective-permute-start = (bf16[1,32,128]{2,0,1:T(2,128)(2,1)S(1)}, bf16[1,32,128]{2,0,1:T(2,128)(2,1)S(1)}, u32[]{:S(2)}, u32[]{:S(2)}) collective-permute-start(bf16[1,32,128]{2,0,1:T(2,128)(2,1)S(1)} %get-tuple-element.40), channel_id=1, source_target_pairs={{0,4},{4,8},{8,12},{12,16},{16,20},{20,24},{24,28},{28,0},{1,5},{5... | collective-permute-start | bytes 24584 | tf_op jit(solution)/shard_map/ppermute | solution.py:16
  11.2 0.7 fusion.119
  11.9 1.7 collective-permute-start.3
  13.7 0.7 collective-permute-done.1
  14.4 1.3 collective-permute-start.2
  15.8 2.1 collective-permute-start.7
  18.8 0.4 pad_maximum_fusion.7
  19.2 0.3 copy.35
  19.5 0.3 copy.41
  19.9 2.6 %collective-permute-start.5 = (bf16[66,1,128]{2,1,0:T(2,128)(2,1)S(1)}, bf16[66,1,128]{2,1,0:T(2,128)(2,1)S(1)}, u32[]{:S(2)}, u32[]{:S(2)}) collective-permute-start(bf16[66,1,128]{2,1,0:T(2,128)(2,1)S(1)} %get-tuple-element.29), channel_id=1, source_target_pairs={{1,0},{2,1},{3,2},{0,3},{5,4},{6,5},{7,6},{4,7},{9,8},{10,9},{11,1... | collective-permute-start | bytes 50696 | tf_op jit(solution)/shard_map/ppermute | solution.py:18
  22.6 0.4 pad_maximum_fusion.1
  23.0 0.6 fusion.116
  23.6 0.3 copy.33
  24.2 0.3 copy.36
  25.6 0.3 copy.42
  26.0 1.2 collective-permute-done.6
  27.2 0.7 pad_maximum_fusion.11
  29.1 0.7 copy-done.4
  32.8 0.4 fusion.21
  33.1 1.4 fusion.43
  35.6 0.3 fusion.38
  35.9 0.4 fusion.37
  36.3 0.3 fusion.36
  36.7 0.3 fusion.35
  37.1 2.0 collective-permute-start.8
  39.1 0.7 collective-permute-start.9
  40.4 1.8 collective-permute-done.9
  42.3 3.6 %collective-permute-start.11 = (bf16[66,1,128]{2,0,1:T(8,128)(2,1)S(1)}, bf16[66,1,128]{2,0,1:T(8,128)(2,1)S(1)}, u32[]{:S(2)}, u32[]{:S(2)}) collective-permute-start(bf16[66,1,128]{2,0,1:T(8,128)(2,1)S(1)} %get-tuple-element.20), channel_id=1, source_target_pairs={{1,0},{2,1},{3,2},{0,3},{5,4},{6,5},{7,6},{4,7},{9,8},{10,9},{11,1... | collective-permute-start | bytes 50696 | tf_op jit(solution)/shard_map/ppermute | solution.py:18
  46.3 0.4 collective-permute-done.10
  46.8 0.4 pad_maximum_fusion.2
  47.2 0.4 fusion.32
  47.6 0.5 fusion.31
  48.1 0.4 fusion.30
  48.5 0.5 fusion.29
  48.9 0.4 fusion.28
  49.3 0.4 fusion.27
  49.7 0.4 fusion.26
  50.2 0.5 fusion.25
  50.7 0.4 fusion.24
  51.1 1.9 pad_maximum_fusion
  53.2 4.3 %copy.91 = f32[1,2,1152,128]{3,1,2,0:T(2,128)S(1)} copy(f32[1,2,1152,128]{3,2,1,0:T(8,128)S(1)} %bitcast.218) | data formatting | bytes 2359296
  57.6 129.3 %all-reduce.2.cloned.1.call-done = f32[2,147456]{1,0:T(2,128)} async-done(((f32[2,147456]{1,0:T(2,128)}), f32[2,147456]{1,0:T(2,128)}) %all-reduce.2.cloned.1.call-update) | async-done | bytes 1179664 | tf_op jit(solution)/shard_map/psum | solution.py:109
  186.8 2.5 %multiply_reduce_fusion = f32[2]{0:T(128)S(1)} fusion(f32[2,147456]{1,0:T(2,128)} %all-reduce.2.cloned.1.call-done), kind=kLoop, calls=%fused_computation.45 | loop fusion | flops 589822 | bytes 1179656 | tf_op jit(solution)/shard_map/reduce_sum | solution.py:110
  189.4 1.3 multiply_add_fusion
  190.8 33.7 %fusion = f32[2,2,147456]{2,0,1:T(2,128)S(1)} fusion(f32[32]{0:T(128)S(1)} %copy-done.8, f32[2,147456]{1,0:T(2,128)S(1)} %bitcast.239, f32[32]{0:T(128)S(1)} %get-tuple-element.43, f32[2,147456]{1,0:T(2,128)S(1)} %get-tuple-element.2, f32[32]{0:T(128)S(1)} %get-tuple-element.44, f32[2,147456]{1,0:T(2,128)S(1)} %get-tuple-element.3, ...), kind=kOutput, calls=%fused_computation.1 | convolution fusion | flops 321454080 | bytes 5899016 | tf_op jit(solution)/shard_map/kh,hlp->klp/dot_general | solution.py:84
  224.5 2.5 %fusion.23 = f32[1,2,147456]{2,0,1:T(1,128)S(1)} fusion(f32[2,2,147456]{2,0,1:T(2,128)S(1)} %fusion), kind=kLoop, calls=%fused_computation.40 | loop fusion | flops 294912 | bytes 3538944 | tf_op jit(solution)/shard_map/mul | solution.py:87
  227.0 2.7 %copy.92 = f32[1,2,147456]{2,1,0:T(2,128)} copy(f32[1,2,147456]{2,0,1:T(1,128)S(1)} %fusion.23) | data formatting | bytes 2359296
  (69 shorter events, 8.9 us)
Async XLA Ops:
  7.2 183.6 %copy-start = (f32[2,32]{1,0:T(2,128)S(1)}, f32[2,32]{1,0:T(2,128)}, u32[]{:S(2)}) copy-start(f32[2,32]{1,0:T(2,128)} %param.14) | copy-start | bytes 772
  7.2 10.7 %copy-start.3 = (bf16[64,32,128]{2,1,0:T(8,128)(2,1)S(1)}, bf16[64,32,128]{2,1,0:T(8,128)(2,1)}, u32[]{:S(2)}) copy-start(bf16[64,32,128]{2,1,0:T(8,128)(2,1)} %param.9) | copy-start | bytes 1572868
  7.2 179.7 %all-reduce.2.cloned.1.call-start = ((), (), s32[]{:S(2)}) async-start(), calls=%async_computation | async-start | bytes 2359296 | tf_op jit(solution)/shard_map/psum | solution.py:109
  8.6 5.1 %collective-permute-start = (bf16[1,32,128]{2,0,1:T(2,128)(2,1)S(1)}, bf16[1,32,128]{2,0,1:T(2,128)(2,1)S(1)}, u32[]{:S(2)}, u32[]{:S(2)}) collective-permute-start(bf16[1,32,128]{2,0,1:T(2,128)(2,1)S(1)} %get-tuple-element.40), channel_id=1, source_target_pairs={{0,4},{4,8},{8,12},{12,16},{16,20},{20,24},{24,28},{28,0},{1,5},{5... | collective-permute-start | bytes 24584 | tf_op jit(solution)/shard_map/ppermute | solution.py:16
  11.2 3.2 %collective-permute-start.1 = (bf16[1,32,128]{2,0,1:T(2,128)(2,1)S(1)}, bf16[1,32,128]{2,0,1:T(2,128)(2,1)S(1)}, u32[]{:S(2)}, u32[]{:S(2)}) collective-permute-start(bf16[1,32,128]{2,0,1:T(2,128)(2,1)S(1)} %get-tuple-element.41), channel_id=1, source_target_pairs={{4,0},{8,4},{12,8},{16,12},{20,16},{24,20},{28,24},{0,28},{5,1},{9... | collective-permute-start | bytes 24584 | tf_op jit(solution)/shard_map/ppermute | solution.py:18
  11.9 5.9 %collective-permute-start.3 = (bf16[1,32,128]{2,1,0:T(8,128)(2,1)S(1)}, bf16[1,32,128]{2,1,0:T(8,128)(2,1)S(1)}, u32[]{:S(2)}, u32[]{:S(2)}) collective-permute-start(bf16[1,32,128]{2,1,0:T(8,128)(2,1)S(1)} %get-tuple-element.35), channel_id=1, source_target_pairs={{0,4},{4,8},{8,12},{12,16},{16,20},{20,24},{24,28},{28,0},{1,5},{5... | collective-permute-start | bytes 24584 | tf_op jit(solution)/shard_map/ppermute | solution.py:16
  13.7 4.2 %collective-permute-start.4 = (bf16[1,32,128]{2,1,0:T(8,128)(2,1)S(1)}, bf16[1,32,128]{2,1,0:T(8,128)(2,1)S(1)}, u32[]{:S(2)}, u32[]{:S(2)}) collective-permute-start(bf16[1,32,128]{2,1,0:T(8,128)(2,1)S(1)} %get-tuple-element.34), channel_id=1, source_target_pairs={{4,0},{8,4},{12,8},{16,12},{20,16},{24,20},{28,24},{0,28},{5,1},{9... | collective-permute-start | bytes 24584 | tf_op jit(solution)/shard_map/ppermute | solution.py:18
  14.4 3.8 %copy-start.2 = (bf16[2,9,128,128]{3,2,1,0:T(8,128)(2,1)S(1)}, bf16[2,9,128,128]{3,2,1,0:T(8,128)(2,1)}, u32[]{:S(2)}) copy-start(bf16[2,9,128,128]{3,2,1,0:T(8,128)(2,1)} %param.10) | copy-start | bytes 1769476
  14.4 8.2 %collective-permute-start.2 = (bf16[66,1,128]{2,0,1:T(8,128)(2,1)S(1)}, bf16[66,1,128]{2,0,1:T(8,128)(2,1)S(1)}, u32[]{:S(2)}, u32[]{:S(2)}) collective-permute-start(bf16[66,1,128]{2,0,1:T(8,128)(2,1)S(1)} %get-tuple-element.25), channel_id=1, source_target_pairs={{0,1},{1,2},{2,3},{3,0},{4,5},{5,6},{6,7},{7,4},{8,9},{9,10},{10,1... | collective-permute-start | bytes 50696 | tf_op jit(solution)/shard_map/ppermute | solution.py:16
  15.8 6.9 %collective-permute-start.7 = (bf16[66,1,128]{2,0,1:T(8,128)(2,1)S(1)}, bf16[66,1,128]{2,0,1:T(8,128)(2,1)S(1)}, u32[]{:S(2)}, u32[]{:S(2)}) collective-permute-start(bf16[66,1,128]{2,0,1:T(8,128)(2,1)S(1)} %get-tuple-element.24), channel_id=1, source_target_pairs={{1,0},{2,1},{3,2},{0,3},{5,4},{6,5},{7,6},{4,7},{9,8},{10,9},{11,1... | collective-permute-start | bytes 50696 | tf_op jit(solution)/shard_map/ppermute | solution.py:18
  19.9 6.1 %collective-permute-start.5 = (bf16[66,1,128]{2,1,0:T(2,128)(2,1)S(1)}, bf16[66,1,128]{2,1,0:T(2,128)(2,1)S(1)}, u32[]{:S(2)}, u32[]{:S(2)}) collective-permute-start(bf16[66,1,128]{2,1,0:T(2,128)(2,1)S(1)} %get-tuple-element.29), channel_id=1, source_target_pairs={{1,0},{2,1},{3,2},{0,3},{5,4},{6,5},{7,6},{4,7},{9,8},{10,9},{11,1... | collective-permute-start | bytes 50696 | tf_op jit(solution)/shard_map/ppermute | solution.py:18
  22.4 4.7 %collective-permute-start.6 = (bf16[66,1,128]{2,1,0:T(2,128)(2,1)S(1)}, bf16[66,1,128]{2,1,0:T(2,128)(2,1)S(1)}, u32[]{:S(2)}, u32[]{:S(2)}) collective-permute-start(bf16[66,1,128]{2,1,0:T(2,128)(2,1)S(1)} %get-tuple-element.30), channel_id=1, source_target_pairs={{0,1},{1,2},{2,3},{3,0},{4,5},{5,6},{6,7},{7,4},{8,9},{9,10},{10,1... | collective-permute-start | bytes 50696 | tf_op jit(solution)/shard_map/ppermute | solution.py:16
  28.8 1.0 copy-start.4
  37.1 3.4 %collective-permute-start.8 = (bf16[1,32,128]{2,0,1:T(2,128)(2,1)S(1)}, bf16[1,32,128]{2,0,1:T(2,128)(2,1)S(1)}, u32[]{:S(2)}, u32[]{:S(2)}) collective-permute-start(bf16[1,32,128]{2,0,1:T(2,128)(2,1)S(1)} %get-tuple-element.36), channel_id=1, source_target_pairs={{0,4},{4,8},{8,12},{12,16},{16,20},{20,24},{24,28},{28,0},{1,5},{5... | collective-permute-start | bytes 24584 | tf_op jit(solution)/shard_map/ppermute | solution.py:16
  39.1 3.2 %collective-permute-start.9 = (bf16[1,32,128]{2,0,1:T(2,128)(2,1)S(1)}, bf16[1,32,128]{2,0,1:T(2,128)(2,1)S(1)}, u32[]{:S(2)}, u32[]{:S(2)}) collective-permute-start(bf16[1,32,128]{2,0,1:T(2,128)(2,1)S(1)} %get-tuple-element.37), channel_id=1, source_target_pairs={{4,0},{8,4},{12,8},{16,12},{20,16},{24,20},{28,24},{0,28},{5,1},{9... | collective-permute-start | bytes 24584 | tf_op jit(solution)/shard_map/ppermute | solution.py:18
  42.3 4.5 %collective-permute-start.10 = (bf16[66,1,128]{2,0,1:T(8,128)(2,1)S(1)}, bf16[66,1,128]{2,0,1:T(8,128)(2,1)S(1)}, u32[]{:S(2)}, u32[]{:S(2)}) collective-permute-start(bf16[66,1,128]{2,0,1:T(8,128)(2,1)S(1)} %get-tuple-element.21), channel_id=1, source_target_pairs={{0,1},{1,2},{2,3},{3,0},{4,5},{5,6},{6,7},{7,4},{8,9},{9,10},{10,1... | collective-permute-start | bytes 50696 | tf_op jit(solution)/shard_map/ppermute | solution.py:16
  42.3 4.5 %collective-permute-start.11 = (bf16[66,1,128]{2,0,1:T(8,128)(2,1)S(1)}, bf16[66,1,128]{2,0,1:T(8,128)(2,1)S(1)}, u32[]{:S(2)}, u32[]{:S(2)}) collective-permute-start(bf16[66,1,128]{2,0,1:T(8,128)(2,1)S(1)} %get-tuple-element.20), channel_id=1, source_target_pairs={{1,0},{2,1},{3,2},{0,3},{5,4},{6,5},{7,6},{4,7},{9,8},{10,9},{11,1... | collective-permute-start | bytes 50696 | tf_op jit(solution)/shard_map/ppermute | solution.py:18
  53.2 4.3 %copy-start.7 = (f32[32,3]{0,1:T(4,128)S(1)}, f32[32,3]{0,1:T(4,128)}, u32[]{:S(2)}) copy-start(f32[32,3]{0,1:T(4,128)} %param.12) | copy-start | bytes 1156
  53.2 136.1 %copy-start.5 = (f32[2,147456]{1,0:T(2,128)S(1)}, f32[2,147456]{1,0:T(2,128)}, u32[]{:S(2)}) copy-start(f32[2,147456]{1,0:T(2,128)} %param.11) | copy-start | bytes 3538948
  186.8 2.5 %copy-start.1 = (f32[2,147456]{1,0:T(2,128)S(1)}, f32[2,147456]{1,0:T(2,128)}, u32[]{:S(2)}) copy-start(f32[2,147456]{1,0:T(2,128)} %all-reduce.2.cloned.1.call-done) | copy-start | bytes 3538948
  189.4 1.4 copy-start.8
  189.4 1.4 copy-start.9
  190.7 33.7 %copy-start.6 = (f32[2,147456]{1,0:T(2,128)}, f32[2,147456]{1,0:T(2,128)S(1)}, u32[]{:S(2)}) copy-start(f32[2,147456]{1,0:T(2,128)S(1)} %get-tuple-element.2) | copy-start | bytes 3538948
Sparse Core Ops, SparseCore 0:
  53.2 133.6 all-reduce.1
where the time goes:
time: 241 us; the launch traced here: 237 us
  waiting for transfers between devices  134 us (56%)
  matrix products  45.9 us (19%)
  starting transfers between devices  17 us (7%)
  between operations  14.8 us (6%)
  local copies, waits for them, and re-layouts  13.3 us (6%)
  other arithmetic  11.9 us (5%)
    psum x1, waiting for transfers between devices, on_device(): grads = lax.psum(local_grads, ('row', 'col'))  129 us
    dot_general x1, matrix products, learned_step(): jnp.einsum('kh,hlp->klp', w_out, units, precision=lax.Precision.HIGHEST)  33.7 us
    unnamed x24, local copies, waits for them, and re-layouts  9.07 us
    ppermute x6, starting transfers between devices, padded_2(): lax.ppermute(head, axis, [((i + 1) % count, i) for i in range(count)])  9.03 us
    ppermute x6, starting transfers between devices, padded_2(): lax.ppermute(tail, axis, [(i, (i + 1) % count) for i in range(count)])  7.95 us
    dot_general x18, matrix products, kernel_grad(): lax.dot_general(window, flat_cot, (((0,), (0,)), ((), ())), preferred_ele...  7.02 us
  transfers between devices with their start and end apart: 13, of which 7 were waited for; matrix products, arithmetic and copies ran while one was open for 5% of the time, Pallas kernels for 0%

commit v1 on v0

v1 whole, which is shorter than its diff:
```python
import functools
import math

import jax
import jax.numpy as jnp
from jax import lax
from jax.experimental import pallas as pl
from jax.experimental.pallas import tpu as pltpu
from jax.sharding import PartitionSpec as P

MESH = pl.DeviceIdType.MESH
TILE = 8
F32 = jnp.float32
BF16 = jnp.bfloat16


def plan(rows_axis, cols_axis, channels):
    bits = rows_axis.bit_length() - 1
    owners = (rows_axis // 2) * cols_axis
    true = (5 * channels, 4 * channels)
    padded = tuple(-(-t // (owners * TILE)) * owners * TILE for t in true)
    orders = (tuple(range(1, bits)), tuple(reversed(range(1, bits))))
    chunks = tuple(p // owners for p in padded)
    return true, padded, orders, chunks


def place(row, order, total):
    off = 0
    for bit in order:
        total //= 2
        off = off + ((row // 2**bit) % 2) * total
    return off


def step_kernel(
    cfg,
    feat, cot, ker, mw, w_in, b_in, w_out, b_out,
    grads_out, upd_out, sq_out,
    edge, ns, we, cr, x3, y3, hid, pg, g, rc, s, rb, zb, sq,
    halo_send, halo_recv, rs_send, rs_recv, z_send, z_recv, sq_send, sq_recv,
    ag_send, ag_recv, agz_send, agz_recv,
):
    rows_axis, cols_axis, param_count, true, padded, orders, chunks = cfg
    tile_rows, tile_cols, ch = feat.shape
    cells = tile_rows * tile_cols
    row, col = lax.axis_index("row"), lax.axis_index("col")
    core = row % 2
    other = row + 1 - 2 * core
    devices = rows_axis * cols_axis
    base = (0, padded[0])

    def remote(src, dst, send, recv, to):
        return pltpu.make_async_remote_copy(
            src_ref=src, dst_ref=dst, send_sem=send, recv_sem=recv,
            device_id=to, device_id_type=MESH,
        )

    for i, ref in enumerate((feat, cot)):
        edge[i, 0] = ref[:, 0:16, :].astype(F32)[:, 0, :].astype(BF16)
        edge[i, 1] = ref[:, tile_cols - 16 :, :].astype(F32)[:, 15, :].astype(BF16)

    barrier = pltpu.get_barrier_semaphore()
    here = row * cols_axis + col

    def greet(d, carry):
        t = (here + d) % devices
        pl.semaphore_signal(
            barrier, inc=1, device_id=(t // cols_axis, t % cols_axis), device_id_type=MESH
        )
        return carry

    lax.fori_loop(1, devices, greet, 0)
    pl.semaphore_wait(barrier, devices - 1)

    up, down = (row + rows_axis - 1) % rows_axis, (row + 1) % rows_axis
    west, east = (col + cols_axis - 1) % cols_axis, (col + 1) % cols_axis
    last = tile_rows - 1
    halos = []
    for i, ref in enumerate((feat, cot)):
        lo, hi = pl.ds(0, 16), pl.ds(tile_cols - 16, 16)
        moves = (
            (ref.at[last], ns.at[i, 0], (down, col)),
            (ref.at[0], ns.at[i, 1], (up, col)),
            (edge.at[i, 1], we.at[i, 0], (row, east)),
            (edge.at[i, 0], we.at[i, 1], (row, west)),
            (ref.at[last, hi], cr.at[i, 0], (down, east)),
            (ref.at[last, lo], cr.at[i, 1], (down, west)),
            (ref.at[0, hi], cr.at[i, 2], (up, east)),
            (ref.at[0, lo], cr.at[i, 3], (up, west)),
        )
        mine = [
            remote(src, dst, halo_send.at[i, k], halo_recv.at[i, k], to)
            for k, (src, dst, to) in enumerate(moves)
        ]
        for copy in mine:
            copy.start()
        halos.append(mine)

    def put(dst, first, v, w, e):
        n = v.shape[0]
        at = lax.broadcasted_iota(jnp.int32, v.shape, 1)
        left = jnp.where(at == 0, w[:, None, :], pltpu.roll(v, 1, 1))
        right = jnp.where(at == tile_cols - 1, e[:, None, :], pltpu.roll(v, tile_cols - 1, 1))
        span = pl.ds(first * tile_cols, n * tile_cols)
        for b, part in enumerate((left, v, right)):
            dst[span, b * ch : (b + 1) * ch] = part.reshape(n * tile_cols, ch).astype(BF16)

    def build(i, ref, dst):
        for copy in halos[i]:
            copy.wait_recv()
        put(dst, 0, ns[i, 0].astype(F32)[None], cr[i, 0].astype(F32)[15:16], cr[i, 1].astype(F32)[0:1])
        for r in range(0, tile_rows, 16):
            span = pl.ds(r, 16)
            put(dst, r + 1, ref[span].astype(F32), we[i, 0, span].astype(F32), we[i, 1, span].astype(F32))
        put(
            dst, tile_rows + 1,
            ns[i, 1].astype(F32)[None], cr[i, 2].astype(F32)[15:16], cr[i, 3].astype(F32)[0:1],
        )

    build(0, feat, x3)
    build(1, cot, y3)

    flip = [
        jnp.concatenate([ker[1, (3 * a + b) * ch : (3 * a + b + 1) * ch] for b in (2, 1, 0)], axis=1)
        for a in range(3)
    ]
    block = min(cells, 512)
    for m in range(0, cells, block):
        pre = jnp.zeros((block, ch), F32)
        back = jnp.zeros((block, ch), F32)
        for a in range(3):
            pre += jnp.dot(
                x3[pl.ds(m + a * tile_cols, block)],
                ker[0, 3 * a * ch : 3 * (a + 1) * ch],
                preferred_element_type=F32,
            )
            back += lax.dot_general(
                y3[pl.ds(m + (2 - a) * tile_cols, block)], flip[a],
                (((1,), (1,)), ((), ())), preferred_element_type=F32,
            )
        sig = 1.0 / (1.0 + jnp.exp(-pre))
        hid[pl.ds(m, block)] = (pre * sig).astype(BF16)
        pg[pl.ds(m, block)] = (back * sig * (1.0 + pre * (1.0 - sig))).astype(BF16)

    def tap_rows(t):
        return pl.ds(t * ch if t < 5 else padded[0] + (t - 5) * ch, ch)

    for part in range(2):
        gap = padded[part] - true[part]
        if gap:
            for layer in range(2):
                g[layer, pl.ds(base[part] + true[part], gap)] = jnp.zeros((gap, ch), F32)

    hid_t, pg_t = hid[...].T, pg[...].T
    for a in range(3):
        two = jnp.dot(hid_t, y3[pl.ds((2 - a) * tile_cols, cells)], preferred_element_type=F32)
        one = jnp.dot(pg_t, x3[pl.ds(a * tile_cols, cells)], preferred_element_type=F32)
        for b in range(3):
            g[1, tap_rows(3 * a + 2 - b)] = two[:, b * ch : (b + 1) * ch]
            g[0, tap_rows(3 * a + b)] = one[:, b * ch : (b + 1) * ch].T

    sent = [copy for mine in halos for copy in mine]
    waits = []
    for part in range(2):
        span = pl.ds(base[part], padded[part])
        copy = remote(
            g.at[1 - core, span], rc.at[span],
            rs_send.at[part, 0], rs_recv.at[part, 0], (other, col),
        )
        copy.start()
        waits.append(copy)
    sent += waits
    off, size, slot = list(base), list(padded), list(base)
    steps = len(orders[0])
    pending = [None, None]

    def begin(part, step):
        bit = orders[part][step]
        side = (row // 2**bit) % 2
        size[part] //= 2
        n = size[part]
        away = pl.multiple_of(off[part] + (1 - side) * n, TILE)
        off[part] = off[part] + side * n
        into = pl.ds(slot[part], n)
        slot[part] += n
        copy = remote(
            s.at[pl.ds(away, n)], rb.at[into],
            rs_send.at[part, step + 1], rs_recv.at[part, step + 1],
            (row + (1 - 2 * side) * 2**bit, col),
        )
        copy.start()
        sent.append(copy)
        pending[part] = (copy, into, n)

    for part in range(2):
        waits[part].wait_recv()
        span = pl.ds(base[part], padded[part])
        s[span] = g[core, span] + rc[span]
        begin(part, 0)
    for step in range(steps):
        for part in range(2):
            copy, into, n = pending[part]
            copy.wait_recv()
            span = pl.ds(pl.multiple_of(off[part], TILE), n)
            s[span] += rb[into]
            if step + 1 < steps:
                begin(part, step + 1)
            else:
                for d in range(1, cols_axis):
                    to = (col + d) % cols_axis
                    n = chunks[part]
                    c = remote(
                        s.at[pl.ds(pl.multiple_of(off[part] + to * n, TILE), n)],
                        zb.at[d, pl.ds(0 if part == 0 else chunks[0], n)],
                        z_send.at[part, d], z_recv.at[part, d], (row, to),
                    )
                    c.start()
                    sent.append(c)
                    pending[part] = (pending[part] if d > 1 else ()) + (c,)

    own = []
    mine = []
    for part in range(2):
        n = chunks[part]
        at = pl.ds(pl.multiple_of(off[part] + col * n, TILE), n)
        total = s[at]
        for d in range(1, cols_axis):
            pending[part][d - 1].wait_recv()
            total += zb[d, pl.ds(0 if part == 0 else chunks[0], n)]
        grads_out[core, at] = total
        own.append(at)
        mine.append(total)

    both = jnp.concatenate(mine, axis=0)
    count = chunks[0] + chunks[1]
    sq[0] = jnp.sum((both * both).reshape(count // TILE, TILE, ch), axis=0)
    owners = (rows_axis // 2) * cols_axis
    me = (row // 2) * cols_axis + col

    def sq_copy(d):
        t = (me + d) % owners
        return remote(
            sq.at[0], sq.at[d], sq_send.at[d], sq_recv.at[d],
            (2 * (t // cols_axis) + core, t % cols_axis),
        )

    def sq_start(d, carry):
        sq_copy(d).start()
        return carry

    lax.fori_loop(1, owners, sq_start, 0)

    def spread_col(k, out):
        copies = []
        for part in range(2):
            for d in range(1, cols_axis):
                c = remote(
                    out.at[core, own[part]], out.at[core, own[part]],
                    agz_send.at[k, part, d], agz_recv.at[k, part, d],
                    (row, (col + d) % cols_axis),
                )
                c.start()
                sent.append(c)
                copies.append((part, c))
        return copies

    outs = (grads_out, upd_out)
    flight = [spread_col(0, grads_out), None]

    def sq_wait(d, tot):
        sq_copy(d).wait_recv()
        return tot + sq[d]

    total = lax.fori_loop(1, owners, sq_wait, sq[0])
    total = jnp.broadcast_to(jnp.sum(total, axis=(0, 1), keepdims=True), (TILE, ch))
    sq_out[core] = total

    norm = 1.0 / jnp.sqrt(total[0:1] / param_count + 1e-06)
    g_hat = both * norm
    mom = 0.9 * mw[0] + 0.1 * g_hat
    scaled = mw[1]

    def unit(h, carry):
        r0, r1 = carry
        v = w_in[h, 0] * g_hat + w_in[h, 1] * mom
        v = v + w_in[h, 2] * scaled + b_in[h]
        u = v * (1.0 / (1.0 + jnp.exp(-v)))
        return r0 + w_out[0, h] * u, r1 + w_out[1, h] * u

    zero = jnp.zeros((count, ch), F32)
    r0, r1 = lax.fori_loop(0, b_in.shape[0], unit, (zero, zero), unroll=4)
    update = (r0 + b_out[0]) * jnp.exp(jnp.tanh(r1 + b_out[1]))
    upd_out[core, own[0]] = update[: chunks[0]]
    upd_out[core, own[1]] = update[chunks[0] :]
    flight[1] = spread_col(1, upd_out)

    sq_final = remote(
        sq_out.at[core], sq_out.at[core], sq_send.at[0], sq_recv.at[0], (other, col)
    )
    sq_final.start()
    sent.append(sq_final)

    offs = [list(off), list(off)]
    sizes = [list(size), list(size)]
    for step in range(steps + 1):
        for k, out in enumerate(outs):
            copies = []
            for part in range(2):
                for p, c in flight[k]:
                    if p == part:
                        c.wait_recv()
                n = sizes[k][part]
                if step < steps:
                    bit = orders[part][steps - 1 - step]
                    side = (row // 2**bit) % 2
                    to = (row + (1 - 2 * side) * 2**bit, col)
                    at = pl.ds(pl.multiple_of(offs[k][part], TILE), n)
                    offs[k][part] = offs[k][part] - side * n
                    sizes[k][part] = 2 * n
                else:
                    to = (other, col)
                    at = pl.ds(base[part], n)
                c = remote(
                    out.at[core, at], out.at[core, at],
                    ag_send.at[k, part, step], ag_recv.at[k, part, step], to,
                )
                c.start()
                sent.append(c)
                copies.append((part, c))
            flight[k] = copies
    for k in range(2):
        for _, c in flight[k]:
            c.wait_recv()
    sq_final.wait_recv()
    for c in sent:
        c.wait_send()

    def sq_done(d, carry):
        sq_copy(d).wait_send()
        return carry

    lax.fori_loop(1, owners, sq_done, 0)


def on_device(
    rows_axis, cols_axis,
    features, cotangent, kernels, momentum, mlp_in_weight, mlp_in_bias, mlp_out_weight, mlp_out_bias,
):
    tile_rows, tile_cols, ch = features.shape
    param_count = 9 * ch * ch
    gain = math.sqrt(9.0 * ch)
    true, padded, orders, chunks = plan(rows_axis, cols_axis, ch)
    row, col = lax.axis_index("row"), lax.axis_index("col")
    steps = len(orders[0])
    owners = (rows_axis // 2) * cols_axis
    length = sum(padded)

    def shard(values):
        pieces, first = [], 0
        for part in range(2):
            size = true[part] * ch
            cut = values[:, first : first + size]
            cut = jnp.pad(cut, ((0, 0), (0, padded[part] * ch - size)))
            at = (place(row, orders[part], padded[part]) + col * chunks[part]) * ch
            piece = lax.dynamic_slice(cut, (row % 2, at), (1, chunks[part] * ch))
            pieces.append(piece.reshape(chunks[part], ch))
            first += size
        return jnp.concatenate(pieces, axis=0).astype(F32)

    mw = jnp.stack([shard(momentum), shard(kernels.reshape(2, param_count)) * gain])
    cfg = (rows_axis, cols_axis, float(param_count), true, padded, orders, chunks)
    vmem = pl.BlockSpec(memory_space=pltpu.VMEM)
    smem = pl.BlockSpec(memory_space=pltpu.SMEM)
    dma = pltpu.SemaphoreType.DMA
    full = (length, ch)
    grads, update, squares = pl.pallas_call(
        functools.partial(step_kernel, cfg),
        out_shape=(
            jax.ShapeDtypeStruct((2,) + full, F32),
            jax.ShapeDtypeStruct((2,) + full, F32),
            jax.ShapeDtypeStruct((2, TILE, ch), F32),
        ),
        in_specs=[vmem] * 4 + [smem] * 4,
        out_specs=(vmem,) * 3,
        scratch_shapes=[
            pltpu.VMEM((2, 2, tile_rows, ch), BF16),
            pltpu.VMEM((2, 2, tile_cols, ch), BF16),
            pltpu.VMEM((2, 2, tile_rows, ch), BF16),
            pltpu.VMEM((2, 4, 16, ch), BF16),
            pltpu.VMEM(((tile_rows + 2) * tile_cols, 3 * ch), BF16),
            pltpu.VMEM(((tile_rows + 2) * tile_cols, 3 * ch), BF16),
            pltpu.VMEM((tile_rows * tile_cols, ch), BF16),
            pltpu.VMEM((tile_rows * tile_cols, ch), BF16),
            pltpu.VMEM((2,) + full, F32),
            pltpu.VMEM(full, F32),
            pltpu.VMEM(full, F32),
            pltpu.VMEM(full, F32),
            pltpu.VMEM((cols_axis, sum(chunks), ch), F32),
            pltpu.VMEM((owners, TILE, ch), F32),
            dma((2, 8)), dma((2, 8)),
            dma((2, steps + 1)), dma((2, steps + 1)),
            dma((2, cols_axis)), dma((2, cols_axis)),
            dma((owners,)), dma((owners,)),
            dma((2, 2, steps + 1)), dma((2, 2, steps + 1)),
            dma((2, 2, cols_axis)), dma((2, 2, cols_axis)),
        ],
        compiler_params=pltpu.CompilerParams(
            collective_id=0, has_side_effects=True, vmem_limit_bytes=48 * 2**20
        ),
    )(
        features, cotangent, kernels.reshape(2, 9 * ch, ch), mw,
        mlp_in_weight, mlp_in_bias, mlp_out_weight, mlp_out_bias,
    )

    def flat(values):
        if padded != true:
            values = jnp.concatenate(
                [values[:, : true[0]], values[:, padded[0] : padded[0] + true[1]]], axis=1
            )
        return values.reshape(2, param_count)

    norm = 1.0 / jnp.sqrt(squares[:, 0, :1] / float(param_count) + 1e-06)
    momentum_out = 0.9 * momentum + 0.1 * (flat(grads) * norm)
    return flat(update), momentum_out


def solution(mesh):
    placed = (P("row", "col", None), P("row", "col", None), P(), P(), P(), P(), P(), P())
    return jax.shard_map(
        functools.partial(on_device, mesh.shape["row"], mesh.shape["col"]),
        mesh=mesh, in_specs=placed, out_specs=(P(), P()), check_vma=False,
    )
```

time: 241 us -> 72.1 us (0.30); the launches traced: 237 us -> 72 us
  waiting for transfers between devices: 134 us -> 0 us
  Pallas kernels: 0 us -> 53.8 us
  matrix products: 45.9 us -> 0 us
  starting transfers between devices: 17 us -> 0 us
  between operations: 14.8 us -> 0.87 us
  other arithmetic: 11.9 us -> 5.25 us
    psum x1 -> x0, waiting for transfers between devices: 129 us -> none  [on_device(): grads = lax.psum(local_grads, ('row', 'col'))]
    pallas_call x0 -> x1, Pallas kernels: none -> 53.8 us  [on_device(): pl.pallas_call(functools.partial(step_kernel, cfg), out_shape=(jax.ShapeD...]
    dot_general x37 -> x0, matrix products: 45.9 us -> none  [the longest x1 33.7 us: learned_step(): jnp.einsum('kh,hlp->klp', w_out, units, precision=lax.Precision.HIGHEST)]
    ppermute x12 -> x0, starting transfers between devices: 17 us -> none  [the longest x6 9.03 us: padded_2(): lax.ppermute(head, axis, [((i + 1) % count, i) for i in range(count)])]
    ppermute x12 -> x0, waiting for transfers between devices: 4.51 us -> none  [the longest x6 2.64 us: padded_2(): lax.ppermute(head, axis, [((i + 1) % count, i) for i in range(count)])]
    add x1, other arithmetic: 1.34 us -> 5.12 us  [on_device(): momentum_out = 0.9 * momentum + 0.1 * (flat(grads) * norm)]
    slice x13 -> x6, local copies, waits for them, and re-layouts: 4.19 us -> 1.44 us  [shard(): cut = values[:, first:first + size]]
    mul x2 -> x1, other arithmetic: 2.63 us -> 0.01 us  [on_device(): shard(kernels.reshape(2, param_count)) * gain]
  transfers between devices with their start and end apart: 13 -> 0, of which waited for: 7 -> 0; matrix products, arithmetic and copies ran while one was open for 5% -> 0% of each run, Pallas kernels for 0% -> 0%
where the time goes in v1:
time: 72.1 us; the launch traced here: 72 us
  Pallas kernels  53.8 us (75%)
  local copies, waits for them, and re-layouts  12.1 us (17%)
  other arithmetic  5.25 us (7%)
  between operations  0.87 us (1%)
    pallas_call x1, Pallas kernels, on_device(): pl.pallas_call(functools.partial(step_kernel, cfg), out_shape=(jax.ShapeD...  53.8 us
    unnamed x19, local copies, waits for them, and re-layouts  10.2 us
    add x1, other arithmetic, on_device(): momentum_out = 0.9 * momentum + 0.1 * (flat(grads) * norm)  5.12 us

profile of v1, /device:TPU:1, one launch (start us, length us, event | category | flops | bytes accessed | tf_op | source)
XLA Modules:
  0.0 72.0 jit_solution(13134136550916569403)
XLA Ops:
  0.6 0.0 slice-start
  0.7 0.0 slice-start.1
  0.7 0.0 copy-start
  0.7 1.0 %slice-done = f32[2,81920]{1,0:T(2,128)S(1)} async-done(((f32[2,147456]{1,0:T(2,128)}), f32[2,81920]{1,0:T(2,128)S(1)}, s32[]{:S(2)}) %slice-start) | async-done | bytes 655384 | tf_op jit(solution)/shard_map/slice | solution.py:362
  1.7 0.1 dynamic_slice.12
  1.9 0.0 slice-done.1
  1.9 0.1 dynamic_slice.13
  2.0 0.1 copy-done
  2.1 0.0 copy-start.7
  2.1 0.0 copy-start.1
  2.1 0.0 copy-start.2
  2.1 0.0 copy-start.3
  2.1 0.0 copy-start.4
  2.1 0.0 copy-start.5
  2.1 4.9 %copy.19 = bf16[1,2,1152,128]{3,1,2,0:T(2,128)(2,1)S(1)} copy(bf16[1,2,1152,128]{3,2,1,0:T(8,128)(2,1)S(1)} %bitcast.23) | data formatting | bytes 1179648
  7.0 0.2 slice.20
  7.3 0.1 dynamic-slice_reduce_fusion
  7.4 0.0 copy-start.6
  7.4 0.2 slice.21
  7.6 0.1 dynamic-slice_reduce_fusion.1
  7.8 0.0 copy-done.7
  7.8 0.1 copy.11.w_in
  7.9 0.0 copy-done.1
  7.9 0.0 copy-done.2
  7.9 0.0 copy-done.3
  7.9 0.0 copy-done.4
  7.9 0.0 copy-done.5
  7.9 53.8 %shard_map.95 = (f32[2,1152,128]{2,1,0:T(8,128)S(1)}, f32[2,1152,128]{2,1,0:T(8,128)S(1)}, f32[2,8,128]{2,1,0:T(8,128)S(1)}) custom-call(bf16[64,32,128]{2,1,0:T(8,128)(2,1)S(1)} %copy-done.1, bf16[64,32,128]{2,1,0:T(8,128)(2,1)S(1)} %copy-done.2, bf16[2,1152,128]{2,1,0:T(8,128)(2,1)S(1)} %bitcast.24, f32[2,72,128]{2,1,0:T(8,128)S(1)} %pad_maximum_fusion.mw, ...), custom_call_target="tpu_custom_call" | custom-call | tf_op jit(solution)/shard_map/pallas_call | solution.py:376
  61.7 0.1 rsqrt_reduce_fusion
  61.8 0.0 copy-done.6
  61.8 5.1 %fusion.1 = f32[2,147456]{1,0:T(2,128)} fusion(f32[1,2,1152,128]{3,2,1,0:T(8,128)S(1)} %bitcast.26, f32[2,147456]{1,0:T(2,128)S(1)} %copy-done.6, f32[2]{0:T(128)S(1)} %rsqrt_reduce_fusion), kind=kLoop, calls=%fused_computation.2 | loop fusion | flops 1179648 | bytes 3538952 | tf_op jit(solution)/shard_map/add | solution.py:423
  66.9 5.1 %copy.18 = f32[1,2,1152,128]{3,1,2,0:T(2,128)} copy(f32[1,2,1152,128]{3,2,1,0:T(8,128)S(1)} %bitcast.25) | data formatting | bytes 2359296
  (3 shorter events, 0.0 us)
Async XLA Ops:
  0.6 1.1 %slice-start = ((f32[2,147456]{1,0:T(2,128)}), f32[2,81920]{1,0:T(2,128)S(1)}, s32[]{:S(2)}) async-start(f32[2,147456]{1,0:T(2,128)} %param.11), calls=%async_computation | async-start | bytes 1310720 | tf_op jit(solution)/shard_map/slice | solution.py:362
  0.7 1.2 %slice-start.1 = ((f32[2,147456]{1,0:T(2,128)}), f32[2,65536]{1,0:T(2,128)S(1)}, s32[]{:S(2)}) async-start(f32[2,147456]{1,0:T(2,128)} %param.11), calls=%async_computation.1 | async-start | bytes 1048576 | tf_op jit(solution)/shard_map/slice | solution.py:362
  0.7 1.3 %copy-start = (bf16[2,9,128,128]{3,2,1,0:T(8,128)(2,1)S(1)}, bf16[2,9,128,128]{3,2,1,0:T(8,128)(2,1)}, u32[]{:S(2)}) copy-start(bf16[2,9,128,128]{3,2,1,0:T(8,128)(2,1)} %param.10) | copy-start | bytes 1769476
  2.1 5.7 %copy-start.7 = (f32[32,3]{0,1:T(4,128)S(1)}, f32[32,3]{0,1:T(4,128)}, u32[]{:S(2)}) copy-start(f32[32,3]{0,1:T(4,128)} %param.12) | copy-start | bytes 1156
  2.1 5.8 %copy-start.1 = (bf16[64,32,128]{2,1,0:T(8,128)(2,1)S(1)}, bf16[64,32,128]{2,1,0:T(8,128)(2,1)}, u32[]{:S(2)}) copy-start(bf16[64,32,128]{2,1,0:T(8,128)(2,1)} %feat.1) | copy-start | bytes 1572868
  2.1 5.8 %copy-start.2 = (bf16[64,32,128]{2,1,0:T(8,128)(2,1)S(1)}, bf16[64,32,128]{2,1,0:T(8,128)(2,1)}, u32[]{:S(2)}) copy-start(bf16[64,32,128]{2,1,0:T(8,128)(2,1)} %cot.1) | copy-start | bytes 1572868
  2.1 5.8 %copy-start.3 = (f32[2,32]{1,0:T(2,128)S(1)}, f32[2,32]{1,0:T(2,128)}, u32[]{:S(2)}) copy-start(f32[2,32]{1,0:T(2,128)} %w_out.1) | copy-start | bytes 772
  2.1 5.8 %copy-start.4 = (f32[32]{0:T(128)S(1)}, f32[32]{0:T(128)}, u32[]{:S(2)}) copy-start(f32[32]{0:T(128)} %b_in.1) | copy-start | bytes 388
  2.1 5.8 %copy-start.5 = (f32[2]{0:T(128)S(1)}, f32[2]{0:T(128)}, u32[]{:S(2)}) copy-start(f32[2]{0:T(128)} %b_out.1) | copy-start | bytes 28
  7.4 54.4 %copy-start.6 = (f32[2,147456]{1,0:T(2,128)S(1)}, f32[2,147456]{1,0:T(2,128)}, u32[]{:S(2)}) copy-start(f32[2,147456]{1,0:T(2,128)} %param.11) | copy-start | bytes 3538948

commit v2 on v1

v2 whole, which is shorter than its diff:
```python
import functools
import math

import jax
import jax.numpy as jnp
from jax import lax
from jax.experimental import pallas as pl
from jax.experimental.pallas import tpu as pltpu
from jax.sharding import PartitionSpec as P

MESH = pl.DeviceIdType.MESH
TILE = 8
F32 = jnp.float32
BF16 = jnp.bfloat16


def plan(rows_axis, cols_axis, channels):
    bits = rows_axis.bit_length() - 1
    owners = (rows_axis // 2) * cols_axis
    true = 3 * channels
    padded = -(-true // (owners * TILE)) * owners * TILE
    stages = list(range(1, bits)) + [None]
    orders = tuple(tuple(stages[p:] + stages[:p]) for p in (0, 1, len(stages) - 1))
    return true, padded, orders, padded // owners


def place(row, col, cols_axis, order, total):
    off = 0
    for bit in order:
        if bit is None:
            total //= cols_axis
            off = off + col * total
        else:
            total //= 2
            off = off + ((row // 2**bit) % 2) * total
    return off


def step_kernel(
    cfg,
    feat, cot, ker, mw, w_in, b_in, w_out, b_out,
    grads_flat, upd_flat, sq_out,
    edge, ns, we, cr, x3, y3, hid, pg, g, rc, s, rb, sq, grads_out, upd_out,
    halo_send, halo_recv, core_send, core_recv, rs_send, rs_recv, sq_send, sq_recv,
    ag_send, ag_recv, fw_send, fw_recv,
):
    rows_axis, cols_axis, param_count, true, padded, orders, chunk = cfg
    tile_rows, tile_cols, ch = feat.shape
    cells = tile_rows * tile_cols
    row, col = lax.axis_index("row"), lax.axis_index("col")
    core = row % 2
    other = row + 1 - 2 * core
    devices = rows_axis * cols_axis
    base = (0, padded, 2 * padded)
    parts = range(3)

    def remote(src, dst, send, recv, to):
        return pltpu.make_async_remote_copy(
            src_ref=src, dst_ref=dst, send_sem=send, recv_sem=recv,
            device_id=to, device_id_type=MESH,
        )

    for i, ref in enumerate((feat, cot)):
        edge[i, 0] = ref[:, 0:16, :].astype(F32)[:, 0, :].astype(BF16)
        edge[i, 1] = ref[:, tile_cols - 16 :, :].astype(F32)[:, 15, :].astype(BF16)

    barrier = pltpu.get_barrier_semaphore()
    here = row * cols_axis + col

    def greet(d, carry):
        t = (here + d) % devices
        pl.semaphore_signal(
            barrier, inc=1, device_id=(t // cols_axis, t % cols_axis), device_id_type=MESH
        )
        return carry

    lax.fori_loop(1, devices, greet, 0)
    pl.semaphore_wait(barrier, devices - 1)

    up, down = (row + rows_axis - 1) % rows_axis, (row + 1) % rows_axis
    west, east = (col + cols_axis - 1) % cols_axis, (col + 1) % cols_axis
    last = tile_rows - 1
    halos = []
    for i, ref in enumerate((feat, cot)):
        lo, hi = pl.ds(0, 16), pl.ds(tile_cols - 16, 16)
        moves = (
            (ref.at[last], ns.at[i, 0], (down, col)),
            (ref.at[0], ns.at[i, 1], (up, col)),
            (edge.at[i, 1], we.at[i, 0], (row, east)),
            (edge.at[i, 0], we.at[i, 1], (row, west)),
            (ref.at[last, hi], cr.at[i, 0], (down, east)),
            (ref.at[last, lo], cr.at[i, 1], (down, west)),
            (ref.at[0, hi], cr.at[i, 2], (up, east)),
            (ref.at[0, lo], cr.at[i, 3], (up, west)),
        )
        mine = [
            remote(src, dst, halo_send.at[i, k], halo_recv.at[i, k], to)
            for k, (src, dst, to) in enumerate(moves)
        ]
        for copy in mine:
            copy.start()
        halos.append(mine)

    def put(dst, first, v, w, e):
        n = v.shape[0]
        at = lax.broadcasted_iota(jnp.int32, v.shape, 1)
        left = jnp.where(at == 0, w[:, None, :], pltpu.roll(v, 1, 1))
        right = jnp.where(at == tile_cols - 1, e[:, None, :], pltpu.roll(v, tile_cols - 1, 1))
        span = pl.ds(first * tile_cols, n * tile_cols)
        for b, part in enumerate((left, v, right)):
            dst[span, b * ch : (b + 1) * ch] = part.reshape(n * tile_cols, ch).astype(BF16)

    def build(i, ref, dst):
        for copy in halos[i]:
            copy.wait_recv()
        put(dst, 0, ns[i, 0].astype(F32)[None], cr[i, 0].astype(F32)[15:16], cr[i, 1].astype(F32)[0:1])
        for r in range(0, tile_rows, 16):
            span = pl.ds(r, 16)
            put(dst, r + 1, ref[span].astype(F32), we[i, 0, span].astype(F32), we[i, 1, span].astype(F32))
        put(
            dst, tile_rows + 1,
            ns[i, 1].astype(F32)[None], cr[i, 2].astype(F32)[15:16], cr[i, 3].astype(F32)[0:1],
        )

    build(0, feat, x3)
    build(1, cot, y3)

    flip = [
        jnp.concatenate([ker[1, (3 * a + b) * ch : (3 * a + b + 1) * ch] for b in (2, 1, 0)], axis=1)
        for a in range(3)
    ]
    block = min(cells, 512)
    for m in range(0, cells, block):
        pre = jnp.zeros((block, ch), F32)
        back = jnp.zeros((block, ch), F32)
        for a in range(3):
            pre += jnp.dot(
                x3[pl.ds(m + a * tile_cols, block)],
                ker[0, 3 * a * ch : 3 * (a + 1) * ch],
                preferred_element_type=F32,
            )
            back += lax.dot_general(
                y3[pl.ds(m + (2 - a) * tile_cols, block)], flip[a],
                (((1,), (1,)), ((), ())), preferred_element_type=F32,
            )
        sig = 1.0 / (1.0 + jnp.exp(-pre))
        hid[pl.ds(m, block)] = (pre * sig).astype(BF16)
        pg[pl.ds(m, block)] = (back * sig * (1.0 + pre * (1.0 - sig))).astype(BF16)

    def tap_rows(t):
        return pl.ds(base[t // 3] + (t % 3) * ch, ch)

    if padded > true:
        for part in parts:
            for layer in range(2):
                g[layer, pl.ds(base[part] + true, padded - true)] = jnp.zeros((padded - true, ch), F32)

    sent = [copy for mine in halos for copy in mine]
    swaps = []
    hid_t, pg_t = hid[...].T, pg[...].T
    for a in parts:
        two = jnp.dot(hid_t, y3[pl.ds((2 - a) * tile_cols, cells)], preferred_element_type=F32)
        one = jnp.dot(pg_t, x3[pl.ds(a * tile_cols, cells)], preferred_element_type=F32)
        for b in range(3):
            g[1, tap_rows(3 * a + 2 - b)] = two[:, b * ch : (b + 1) * ch]
            g[0, tap_rows(3 * a + b)] = one[:, b * ch : (b + 1) * ch].T
        span = pl.ds(base[a], padded)
        copy = remote(
            g.at[1 - core, span], rc.at[span], core_send.at[a], core_recv.at[a], (other, col)
        )
        copy.start()
        swaps.append(copy)
    sent += swaps

    off, size, slot = list(base), [padded] * 3, list(base)
    steps = len(orders[0])
    pending = [None] * 3

    def rows_at(start, n):
        return pl.ds(pl.multiple_of(start, TILE), n)

    def begin(part, step):
        bit = orders[part][step]
        if bit is None:
            n = size[part] // cols_axis
            peers = [
                (d, off[part] + ((col + d) % cols_axis) * n, (row, (col + d) % cols_axis))
                for d in range(1, cols_axis)
            ]
            off[part] = off[part] + col * n
        else:
            n = size[part] // 2
            side = (row // 2**bit) % 2
            peers = [(0, off[part] + (1 - side) * n, (row + (1 - 2 * side) * 2**bit, col))]
            off[part] = off[part] + side * n
        size[part] = n
        pending[part] = []
        for d, start, to in peers:
            into = pl.ds(slot[part], n)
            slot[part] += n
            copy = remote(
                s.at[rows_at(start, n)], rb.at[into],
                rs_send.at[part, step, d], rs_recv.at[part, step, d], to,
            )
            copy.start()
            sent.append(copy)
            pending[part].append((copy, into))

    for part in parts:
        swaps[part].wait_recv()
        span = pl.ds(base[part], padded)
        s[span] = g[core, span] + rc[span]
        begin(part, 0)
    own, mine = [], []
    for step in range(steps):
        for part in parts:
            at = rows_at(off[part], size[part])
            total = s[at]
            for copy, into in pending[part]:
                copy.wait_recv()
                total += rb[into]
            if step + 1 < steps:
                s[at] = total
                begin(part, step + 1)
            else:
                grads_out[core, at] = total
                own.append(at)
                mine.append(total)

    outs = (grads_out, upd_out)
    offs, sizes = [list(off), list(off)], [list(size), list(size)]
    flight = [[None] * 3, [None] * 3]
    landing = [[], []]

    def forward(k, part, step, d, at):
        c = remote(
            outs[k].at[core, at], outs[k].at[core, at],
            fw_send.at[k, part, step, d], fw_recv.at[k, part, step, d], (other, col),
        )
        c.start()
        sent.append(c)
        landing[k].append(c)

    def spread(k, part, step):
        bit = orders[part][step]
        n, first = sizes[k][part], offs[k][part]
        here_at = rows_at(first, n)
        if bit is None:
            whole = first - col * n
            peers = [
                (d, (row, (col + d) % cols_axis), whole + ((col + cols_axis - d) % cols_axis) * n)
                for d in range(1, cols_axis)
            ]
            offs[k][part], sizes[k][part] = whole, n * cols_axis
        else:
            side = (row // 2**bit) % 2
            whole = first - side * n
            peers = [(0, (row + (1 - 2 * side) * 2**bit, col), whole + (1 - side) * n)]
            offs[k][part], sizes[k][part] = whole, 2 * n
        flight[k][part] = []
        for d, to, arrives in peers:
            c = remote(
                outs[k].at[core, here_at], outs[k].at[core, here_at],
                ag_send.at[k, part, step, d], ag_recv.at[k, part, step, d], to,
            )
            c.start()
            sent.append(c)
            flight[k][part].append((c, step, d, rows_at(arrives, n)))

    def collect(k, part):
        for c, step, d, at in flight[k][part]:
            c.wait_recv()
            forward(k, part, step, d, at)

    def launch(k):
        for part in parts:
            spread(k, part, steps - 1)
        for part in parts:
            forward(k, part, steps, 0, own[part])

    both = jnp.concatenate(mine, axis=0)
    count = 3 * chunk
    sq[0] = jnp.sum((both * both).reshape(count // TILE, TILE, ch), axis=0)
    owners = (rows_axis // 2) * cols_axis
    me = (row // 2) * cols_axis + col

    def sq_copy(d):
        t = (me + d) % owners
        return remote(
            sq.at[0], sq.at[d], sq_send.at[d], sq_recv.at[d],
            (2 * (t // cols_axis) + core, t % cols_axis),
        )

    def sq_start(d, carry):
        sq_copy(d).start()
        return carry

    lax.fori_loop(1, owners, sq_start, 0)

    launch(0)

    def sq_wait(d, tot):
        sq_copy(d).wait_recv()
        return tot + sq[d]

    total = lax.fori_loop(1, owners, sq_wait, sq[0])
    total = jnp.broadcast_to(jnp.sum(total, axis=(0, 1), keepdims=True), (TILE, ch))
    sq_out[core] = total

    norm = 1.0 / jnp.sqrt(total[0:1] / param_count + 1e-06)
    g_hat = both * norm
    mom = 0.9 * mw[0] + 0.1 * g_hat
    scaled = mw[1]

    def unit(h, carry):
        r0, r1 = carry
        v = w_in[h, 0] * g_hat + w_in[h, 1] * mom
        v = v + w_in[h, 2] * scaled + b_in[h]
        u = v * (1.0 / (1.0 + jnp.exp(-v)))
        return r0 + w_out[0, h] * u, r1 + w_out[1, h] * u

    zero = jnp.zeros((count, ch), F32)
    r0, r1 = lax.fori_loop(0, b_in.shape[0], unit, (zero, zero), unroll=4)
    update = (r0 + b_out[0]) * jnp.exp(jnp.tanh(r1 + b_out[1]))
    for part in parts:
        upd_out[core, own[part]] = update[part * chunk : (part + 1) * chunk]
    launch(1)

    sq_final = remote(
        sq_out.at[core], sq_out.at[core], sq_send.at[0], sq_recv.at[0], (other, col)
    )
    sq_final.start()
    sent.append(sq_final)

    for step in reversed(range(steps)):
        for k in range(2):
            for part in parts:
                collect(k, part)
                if step > 0:
                    spread(k, part, step - 1)
    for k, flat in enumerate((grads_flat, upd_flat)):
        for c in landing[k]:
            c.wait_recv()
        for layer in range(2):
            for part in parts:
                flat[pl.ds(2 * part * true + layer, true, stride=2), :] = outs[k][
                    layer, pl.ds(base[part], true)
                ]
    sq_final.wait_recv()
    for c in sent:
        c.wait_send()

    def sq_done(d, carry):
        sq_copy(d).wait_send()
        return carry

    lax.fori_loop(1, owners, sq_done, 0)


def on_device(
    rows_axis, cols_axis,
    features, cotangent, kernels, momentum, mlp_in_weight, mlp_in_bias, mlp_out_weight, mlp_out_bias,
):
    tile_rows, tile_cols, ch = features.shape
    param_count = 9 * ch * ch
    gain = math.sqrt(9.0 * ch)
    true, padded, orders, chunk = plan(rows_axis, cols_axis, ch)
    row, col = lax.axis_index("row"), lax.axis_index("col")
    steps = len(orders[0])
    owners = (rows_axis // 2) * cols_axis
    length = 3 * padded

    def shard(values, unit):
        pieces = []
        for part in range(3):
            at = place(row, col, cols_axis, orders[part], padded)
            if padded > true:
                cut = values[:, part * true * unit : (part + 1) * true * unit]
                pads = ((0, 0), (0, (padded - true) * unit)) + ((0, 0),) * (values.ndim - 2)
                cut = jnp.pad(cut, pads)
            else:
                cut, at = values, at + part * true
            start = (row % 2, at * unit) + (0,) * (values.ndim - 2)
            piece = lax.dynamic_slice(cut, start, (1, chunk * unit) + values.shape[2:])
            pieces.append(piece.reshape(chunk, ch).astype(F32))
        return jnp.concatenate(pieces, axis=0)

    mw = jnp.stack([shard(momentum, ch), shard(kernels.reshape(2, 9 * ch, ch), 1) * gain])
    cfg = (rows_axis, cols_axis, float(param_count), true, padded, orders, chunk)
    vmem = pl.BlockSpec(memory_space=pltpu.VMEM)
    smem = pl.BlockSpec(memory_space=pltpu.SMEM)
    dma = pltpu.SemaphoreType.DMA
    full = (length, ch)
    grads, update, squares = pl.pallas_call(
        functools.partial(step_kernel, cfg),
        out_shape=(
            jax.ShapeDtypeStruct((18 * ch, ch), F32),
            jax.ShapeDtypeStruct((18 * ch, ch), F32),
            jax.ShapeDtypeStruct((2, TILE, ch), F32),
        ),
        in_specs=[vmem] * 4 + [smem] * 4,
        out_specs=(vmem,) * 3,
        scratch_shapes=[
            pltpu.VMEM((2, 2, tile_rows, ch), BF16),
            pltpu.VMEM((2, 2, tile_cols, ch), BF16),
            pltpu.VMEM((2, 2, tile_rows, ch), BF16),
            pltpu.VMEM((2, 4, 16, ch), BF16),
            pltpu.VMEM(((tile_rows + 2) * tile_cols, 3 * ch), BF16),
            pltpu.VMEM(((tile_rows + 2) * tile_cols, 3 * ch), BF16),
            pltpu.VMEM((tile_rows * tile_cols, ch), BF16),
            pltpu.VMEM((tile_rows * tile_cols, ch), BF16),
            pltpu.VMEM((2,) + full, F32),
            pltpu.VMEM(full, F32),
            pltpu.VMEM(full, F32),
            pltpu.VMEM(full, F32),
            pltpu.VMEM((owners, TILE, ch), F32),
            pltpu.VMEM((2,) + full, F32),
            pltpu.VMEM((2,) + full, F32),
            dma((2, 8)), dma((2, 8)),
            dma((3,)), dma((3,)),
            dma((3, steps, cols_axis)), dma((3, steps, cols_axis)),
            dma((owners,)), dma((owners,)),
            dma((2, 3, steps, cols_axis)), dma((2, 3, steps, cols_axis)),
            dma((2, 3, steps + 1, cols_axis)), dma((2, 3, steps + 1, cols_axis)),
        ],
        compiler_params=pltpu.CompilerParams(
            collective_id=0, has_side_effects=True, vmem_limit_bytes=48 * 2**20
        ),
    )(
        features, cotangent, kernels.reshape(2, 9 * ch, ch), mw,
        mlp_in_weight, mlp_in_bias, mlp_out_weight, mlp_out_bias,
    )

    def flat(values):
        return values.reshape(9 * ch, 2, ch).transpose(1, 0, 2).reshape(2, param_count)

    norm = 1.0 / jnp.sqrt(squares[:, 0, :1] / float(param_count) + 1e-06)
    momentum_out = 0.9 * momentum + 0.1 * (flat(grads) * norm)
    return flat(update), momentum_out


def solution(mesh):
    placed = (P("row", "col", None), P("row", "col", None), P(), P(), P(), P(), P(), P())
    return jax.shard_map(
        functools.partial(on_device, mesh.shape["row"], mesh.shape["col"]),
        mesh=mesh, in_specs=placed, out_specs=(P(), P()), check_vma=False,
    )
```

time: 72.1 us -> 68 us (0.943)
  local copies, waits for them, and re-layouts: 12.1 us -> 8.57 us
  other arithmetic: 5.25 us -> 2.07 us
  Pallas kernels: 53.8 us -> 56.1 us
    unnamed x19 -> x16, local copies, waits for them, and re-layouts: 10.2 us -> 6.91 us
    add x1, other arithmetic: 5.12 us -> 1.94 us  [on_device(): momentum_out = 0.9 * momentum + 0.1 * (flat(grads) * norm)]
    pallas_call x1, Pallas kernels: 53.8 us -> 56.1 us  [on_device(): pl.pallas_call(functools.partial(step_kernel, cfg), out_shape=(jax.ShapeD...]
    slice x6 -> x0, local copies, waits for them, and re-layouts: 1.44 us -> none  [shard(): cut = values[:, first:first + size]]
    dynamic_slice x4 -> x2, local copies, waits for them, and re-layouts: 0.48 us -> 1.66 us  [shard(): piece = lax.dynamic_slice(cut, start, (1, chunk * unit) + values.shape[2:])]
where the time goes in v2:
time: 68 us; the launch traced here: 67.6 us
  Pallas kernels  56.1 us (82%)
  local copies, waits for them, and re-layouts  8.57 us (13%)
  other arithmetic  2.07 us (3%)
  between operations  0.77 us (1%)
    pallas_call x1, Pallas kernels, on_device(): pl.pallas_call(functools.partial(step_kernel, cfg), out_shape=(jax.ShapeD...  56.1 us
    unnamed x16, local copies, waits for them, and re-layouts  6.91 us
    add x1, other arithmetic, on_device(): momentum_out = 0.9 * momentum + 0.1 * (flat(grads) * norm)  1.94 us
    dynamic_slice x2, local copies, waits for them, and re-layouts, shard(): piece = lax.dynamic_slice(cut, start, (1, chunk * unit) + values.shape[2:])  1.66 us

profile of v2, /device:TPU:1, one launch (start us, length us, event | category | flops | bytes accessed | tf_op | source)
XLA Modules:
  0.0 67.6 jit_solution(957791323496790997)
XLA Ops:
  0.7 0.9 %fusion = (f32[1,3072]{1,0:T(1,128)S(1)}, f32[1,3072]{1,0:T(1,128)S(1)}, f32[1,3072]{1,0:T(1,128)S(1)}) fusion(f32[2,147456]{1,0:T(2,128)} %param.11, s32[]{:T(128)S(6)} %select_n.89, s32[]{:T(128)S(6)} %select_n.94, s32[]{:T(128)S(6)} %select_n.95, s32[]{:T(128)S(6)} %select_n.96), kind=kLoop, calls=%fused_computation.8 | loop fusion | bytes 73744 | tf_op jit(solution)/shard_map/dynamic_slice | solution.py:384
  1.7 0.7 %constant_dynamic-slice_fusion.2 = (bf16[1,24,128]{2,1,0:T(8,128)(2,1)S(1)}, bf16[1,24,128]{2,1,0:T(8,128)(2,1)S(1)}, bf16[1,24,128]{2,1,0:T(8,128)(2,1)S(1)}) fusion(bf16[2,1152,128]{2,1,0:T(8,128)(2,1)} %bitcast.18, s32[]{:T(128)S(6)} %select_n.89, s32[]{:T(128)S(6)} %select_n.97, s32[]{:T(128)S(6)} %select_n.99, s32[]{:T(128)S(6)} %select_n.98), kind=kLoop, calls=%fused_computation.7 | loop fusion | bytes 36880 | tf_op jit(solution)/shard_map/dynamic_slice | solution.py:384
  2.4 0.8 %copy.13.w_in = f32[32,3]{1,0:T(8,128)S(1)} copy(f32[32,3]{0,1:T(4,128)} %param.12) | data formatting | bytes 768 | tf_op args[4]
  3.2 0.0 copy-start
  3.2 1.1 %copy-done = bf16[2,9,128,128]{3,2,1,0:T(8,128)(2,1)S(1)} copy-done((bf16[2,9,128,128]{3,2,1,0:T(8,128)(2,1)S(1)}, bf16[2,9,128,128]{3,2,1,0:T(8,128)(2,1)}, u32[]{:S(2)}) %copy-start) | copy-done | bytes 589848
  4.3 0.0 copy-start.1
  4.3 1.0 %copy-done.1 = bf16[64,32,128]{2,1,0:T(8,128)(2,1)S(1)} copy-done((bf16[64,32,128]{2,1,0:T(8,128)(2,1)S(1)}, bf16[64,32,128]{2,1,0:T(8,128)(2,1)}, u32[]{:S(2)}) %copy-start.1) | copy-done | bytes 524312
  5.3 0.0 copy-start.2
  5.3 1.0 %copy-done.2 = bf16[64,32,128]{2,1,0:T(8,128)(2,1)S(1)} copy-done((bf16[64,32,128]{2,1,0:T(8,128)(2,1)S(1)}, bf16[64,32,128]{2,1,0:T(8,128)(2,1)}, u32[]{:S(2)}) %copy-start.2) | copy-done | bytes 524312
  6.3 0.0 copy-start.3
  6.3 0.7 %copy-done.3 = f32[2,32]{1,0:T(2,128)S(1)} copy-done((f32[2,32]{1,0:T(2,128)S(1)}, f32[2,32]{1,0:T(2,128)}, u32[]{:S(2)}) %copy-start.3) | copy-done | bytes 280
  7.0 0.0 copy-start.4
  7.0 0.7 copy-done.4
  7.7 0.0 copy-start.5
  7.7 0.7 copy-done.5
  8.3 0.0 copy-start.6
  8.3 56.1 %shard_map.95 = (f32[2304,128]{1,0:T(8,128)S(1)}, f32[2304,128]{1,0:T(8,128)S(1)}, f32[2,8,128]{2,1,0:T(8,128)S(1)}) custom-call(bf16[64,32,128]{2,1,0:T(8,128)(2,1)S(1)} %copy-done.1, bf16[64,32,128]{2,1,0:T(8,128)(2,1)S(1)} %copy-done.2, bf16[2,1152,128]{2,1,0:T(8,128)(2,1)S(1)} %bitcast.19, f32[2,72,128]{2,1,0:T(8,128)S(1)} %pad_maximum_fusion.mw, ...), custom_call_target="tpu_custom_call" | custom-call | tf_op jit(solution)/shard_map/pallas_call | solution.py:394
  64.5 0.1 rsqrt_reduce_fusion
  64.6 0.0 copy-done.6
  64.6 1.9 %multiply_add_fusion = f32[2,147456]{1,0:T(2,128)} fusion(f32[2,147456]{1,0:T(2,128)S(1)} %bitcast.17, f32[2,147456]{1,0:T(2,128)S(1)} %copy-done.6, f32[2]{0:T(128)S(1)} %rsqrt_reduce_fusion), kind=kLoop, calls=%fused_computation | loop fusion | flops 1179648 | bytes 3538952 | tf_op jit(solution)/shard_map/add | solution.py:438
  66.5 1.0 %copy.17 = f32[2,147456]{1,0:T(2,128)} copy(f32[2,147456]{1,0:T(2,128)S(1)} %bitcast.16) | data formatting | bytes 2359296
  (3 shorter events, 0.0 us)
Async XLA Ops:
  3.2 1.1 %copy-start = (bf16[2,9,128,128]{3,2,1,0:T(8,128)(2,1)S(1)}, bf16[2,9,128,128]{3,2,1,0:T(8,128)(2,1)}, u32[]{:S(2)}) copy-start(bf16[2,9,128,128]{3,2,1,0:T(8,128)(2,1)} %param.10) | copy-start | bytes 1769476
  4.3 1.0 %copy-start.1 = (bf16[64,32,128]{2,1,0:T(8,128)(2,1)S(1)}, bf16[64,32,128]{2,1,0:T(8,128)(2,1)}, u32[]{:S(2)}) copy-start(bf16[64,32,128]{2,1,0:T(8,128)(2,1)} %feat.1) | copy-start | bytes 1572868
  5.3 1.0 %copy-start.2 = (bf16[64,32,128]{2,1,0:T(8,128)(2,1)S(1)}, bf16[64,32,128]{2,1,0:T(8,128)(2,1)}, u32[]{:S(2)}) copy-start(bf16[64,32,128]{2,1,0:T(8,128)(2,1)} %cot.1) | copy-start | bytes 1572868
  6.3 0.7 %copy-start.3 = (f32[2,32]{1,0:T(2,128)S(1)}, f32[2,32]{1,0:T(2,128)}, u32[]{:S(2)}) copy-start(f32[2,32]{1,0:T(2,128)} %w_out.1) | copy-start | bytes 772
  7.0 0.7 copy-start.4
  7.7 0.7 copy-start.5
  8.3 56.3 %copy-start.6 = (f32[2,147456]{1,0:T(2,128)S(1)}, f32[2,147456]{1,0:T(2,128)}, u32[]{:S(2)}) copy-start(f32[2,147456]{1,0:T(2,128)} %param.11) | copy-start | bytes 3538948

commit v3 on v2

--- a/solution.py
+++ b/solution.py
@@ -38,8 +38,9 @@
 
 def step_kernel(
     cfg,
-    feat, cot, ker, mw, w_in, b_in, w_out, b_out,
+    feat_hbm, cot_hbm, ker_hbm, mom_hbm, w_in_hbm, b_in_hbm, w_out_hbm, b_out_hbm,
     grads_flat, upd_flat, sq_out,
+    feat, cot, ker, mom_in, ker_in, w_in, b_in, w_out, b_out, load_sem,
     edge, ns, we, cr, x3, y3, hid, pg, g, rc, s, rb, sq, grads_out, upd_out,
     halo_send, halo_recv, core_send, core_recv, rs_send, rs_recv, sq_send, sq_recv,
     ag_send, ag_recv, fw_send, fw_recv,
@@ -60,6 +61,29 @@
             device_id=to, device_id_type=MESH,
         )
 
+    loads = [
+        pltpu.make_async_copy(src, dst, load_sem.at[i])
+        for i, (src, dst) in enumerate((
+            (feat_hbm, feat), (cot_hbm, cot), (ker_hbm, ker), (w_in_hbm, w_in),
+            (b_in_hbm, b_in), (w_out_hbm, w_out), (b_out_hbm, b_out),
+        ))
+    ]
+    for part in parts:
+        at = place(row, col, cols_axis, orders[part], padded)
+        if padded > true:
+            at = at % true
+        at = pl.multiple_of(part * true + at, TILE)
+        twice = pl.multiple_of(2 * at, 2 * TILE)
+        loads.append(pltpu.make_async_copy(
+            mom_hbm.at[pl.ds(twice, 2 * chunk)], mom_in.at[part], load_sem.at[7 + part]
+        ))
+        loads.append(pltpu.make_async_copy(
+            ker_hbm.at[core, pl.ds(at, chunk)], ker_in.at[part], load_sem.at[10 + part]
+        ))
+    for copy in loads:
+        copy.start()
+    for copy in loads[:2]:
+        copy.wait()
     for i, ref in enumerate((feat, cot)):
         edge[i, 0] = ref[:, 0:16, :].astype(F32)[:, 0, :].astype(BF16)
         edge[i, 1] = ref[:, tile_cols - 16 :, :].astype(F32)[:, 15, :].astype(BF16)
@@ -125,6 +149,7 @@
     build(0, feat, x3)
     build(1, cot, y3)
 
+    loads[2].wait()
     flip = [
         jnp.concatenate([ker[1, (3 * a + b) * ch : (3 * a + b + 1) * ch] for b in (2, 1, 0)], axis=1)
         for a in range(3)
@@ -307,15 +332,21 @@
     total = jnp.broadcast_to(jnp.sum(total, axis=(0, 1), keepdims=True), (TILE, ch))
     sq_out[core] = total
 
+    for copy in loads[3:]:
+        copy.wait()
+    momentum = jnp.concatenate(
+        [mom_in[part, pl.ds(core, chunk, stride=2), :] for part in parts], axis=0
+    )
+    scaled = jnp.concatenate([ker_in[part].astype(F32) for part in parts], axis=0)
+    scaled = scaled * math.sqrt(9.0 * ch)
     norm = 1.0 / jnp.sqrt(total[0:1] / param_count + 1e-06)
     g_hat = both * norm
-    mom = 0.9 * mw[0] + 0.1 * g_hat
-    scaled = mw[1]
+    mom = 0.9 * momentum + 0.1 * g_hat
 
     def unit(h, carry):
         r0, r1 = carry
-        v = w_in[h, 0] * g_hat + w_in[h, 1] * mom
-        v = v + w_in[h, 2] * scaled + b_in[h]
+        v = w_in[0, h] * g_hat + w_in[1, h] * mom
+        v = v + w_in[2, h] * scaled + b_in[h]
         u = v * (1.0 / (1.0 + jnp.exp(-v)))
         return r0 + w_out[0, h] * u, r1 + w_out[1, h] * u
 
@@ -363,32 +394,15 @@
 ):
     tile_rows, tile_cols, ch = features.shape
     param_count = 9 * ch * ch
-    gain = math.sqrt(9.0 * ch)
     true, padded, orders, chunk = plan(rows_axis, cols_axis, ch)
-    row, col = lax.axis_index("row"), lax.axis_index("col")
     steps = len(orders[0])
     owners = (rows_axis // 2) * cols_axis
     length = 3 * padded
 
-    def shard(values, unit):
-        pieces = []
-        for part in range(3):
-            at = place(row, col, cols_axis, orders[part], padded)
-            if padded > true:
-                cut = values[:, part * true * unit : (part + 1) * true * unit]
-                pads = ((0, 0), (0, (padded - true) * unit)) + ((0, 0),) * (values.ndim - 2)
-                cut = jnp.pad(cut, pads)
-            else:
-                cut, at = values, at + part * true
-            start = (row % 2, at * unit) + (0,) * (values.ndim - 2)
-            piece = lax.dynamic_slice(cut, start, (1, chunk * unit) + values.shape[2:])
-            pieces.append(piece.reshape(chunk, ch).astype(F32))
-        return jnp.concatenate(pieces, axis=0)
-
-    mw = jnp.stack([shard(momentum, ch), shard(kernels.reshape(2, 9 * ch, ch), 1) * gain])
     cfg = (rows_axis, cols_axis, float(param_count), true, padded, orders, chunk)
     vmem = pl.BlockSpec(memory_space=pltpu.VMEM)
-    smem = pl.BlockSpec(memory_space=pltpu.SMEM)
+    hbm = pl.BlockSpec(memory_space=pltpu.HBM)
+    hidden_units = mlp_in_bias.shape[0]
     dma = pltpu.SemaphoreType.DMA
     full = (length, ch)
     grads, update, squares = pl.pallas_call(
@@ -398,9 +412,19 @@
             jax.ShapeDtypeStruct((18 * ch, ch), F32),
             jax.ShapeDtypeStruct((2, TILE, ch), F32),
         ),
-        in_specs=[vmem] * 4 + [smem] * 4,
+        in_specs=[hbm] * 8,
         out_specs=(vmem,) * 3,
         scratch_shapes=[
+            pltpu.VMEM(features.shape, BF16),
+            pltpu.VMEM(cotangent.shape, BF16),
+            pltpu.VMEM((2, 9 * ch, ch), BF16),
+            pltpu.VMEM((3, 2 * chunk, ch), F32),
+            pltpu.VMEM((3, chunk, ch), BF16),
+            pltpu.SMEM((3, hidden_units), F32),
+            pltpu.SMEM((hidden_units,), F32),
+            pltpu.SMEM((2, hidden_units), F32),
+            pltpu.SMEM((2,), F32),
+            dma((13,)),
             pltpu.VMEM((2, 2, tile_rows, ch), BF16),
             pltpu.VMEM((2, 2, tile_cols, ch), BF16),
             pltpu.VMEM((2, 2, tile_rows, ch), BF16),
@@ -424,11 +448,12 @@
             dma((2, 3, steps + 1, cols_axis)), dma((2, 3, steps + 1, cols_axis)),
         ],
         compiler_params=pltpu.CompilerParams(
-            collective_id=0, has_side_effects=True, vmem_limit_bytes=48 * 2**20
+            collective_id=0, has_side_effects=True, vmem_limit_bytes=64600000
         ),
     )(
-        features, cotangent, kernels.reshape(2, 9 * ch, ch), mw,
-        mlp_in_weight, mlp_in_bias, mlp_out_weight, mlp_out_bias,
+        features, cotangent, kernels.reshape(2, 9 * ch, ch),
+        momentum.reshape(2, 9 * ch, ch).transpose(1, 0, 2).reshape(18 * ch, ch),
+        mlp_in_weight.T, mlp_in_bias, mlp_out_weight, mlp_out_bias,
     )
 
     def flat(values):

time: 68 us -> 64.4 us (0.947)
  local copies, waits for them, and re-layouts: 8.57 us -> 1.02 us
  Pallas kernels: 56.1 us -> 58.6 us
  other arithmetic: 2.07 us -> 3.89 us
    unnamed x16 -> x5, local copies, waits for them, and re-layouts: 6.91 us -> 1.02 us
    pallas_call x1, Pallas kernels: 56.1 us -> 58.6 us  [on_device(): pl.pallas_call(functools.partial(step_kernel, cfg), out_shape=(jax.ShapeD...]
    dynamic_slice x2 -> x0, local copies, waits for them, and re-layouts: 1.66 us -> none  [shard(): piece = lax.dynamic_slice(cut, start, (1, chunk * unit) + values.shape[2:])]
    add x1, other arithmetic: 1.94 us -> 3.09 us  [on_device(): momentum_out = 0.9 * momentum + 0.1 * (flat(grads) * norm)]
    sqrt x1, other arithmetic: 0.1 us -> 0.8 us  [on_device(): norm = 1.0 / jnp.sqrt(squares[:, 0, :1] / float(param_count) + 1e-06)]
where the time goes in v3:
time: 64.4 us; the launch traced here: 64.2 us
  Pallas kernels  58.6 us (91%)
  other arithmetic  3.89 us (6%)
  local copies, waits for them, and re-layouts  1.02 us (2%)
  between operations  0.65 us (1%)
    pallas_call x1, Pallas kernels, on_device(): pl.pallas_call(functools.partial(step_kernel, cfg), out_shape=(jax.ShapeD...  58.6 us
    add x1, other arithmetic, on_device(): momentum_out = 0.9 * momentum + 0.1 * (flat(grads) * norm)  3.09 us

profile of v3, /device:TPU:1, one launch (start us, length us, event | category | flops | bytes accessed | tf_op | source)
XLA Modules:
  0.0 64.2 jit_solution(1691867975615130869)
XLA Ops:
  0.6 0.0 copy-start
  0.6 58.6 %shard_map.95 = (f32[2304,128]{1,0:T(8,128)}, f32[2304,128]{1,0:T(8,128)}, f32[2,8,128]{2,1,0:T(8,128)}) custom-call(bf16[64,32,128]{2,1,0:T(8,128)(2,1)} %feat_hbm.1, bf16[64,32,128]{2,1,0:T(8,128)(2,1)} %cot_hbm.1, bf16[2,1152,128]{2,1,0:T(8,128)(2,1)} %bitcast.20, f32[2304,128]{1,0:T(8,128)} %bitcast.17, f32[3,32]{1,0:T(4,128)} %bitcast.21, f32[32]{0:T(128)} %b_in_hbm.1, ...), custom_call_target="tpu_custom_call" | custom-call | tf_op jit(solution)/shard_map/pallas_call | solution.py:408
  59.3 0.8 %rsqrt_reduce_fusion = f32[2]{0:T(128)S(1)} fusion(f32[2,8,128]{2,1,0:T(8,128)} %get-tuple-element.7), kind=kLoop, calls=%fused_computation.1 | loop fusion | flops 4 | bytes 16 | tf_op jit(solution)/shard_map/sqrt | solution.py:462
  60.1 0.0 copy-done
  60.1 0.0 copy-start.1
  60.1 3.1 %multiply_add_fusion = f32[2,147456]{1,0:T(2,128)} fusion(f32[2,147456]{1,0:T(2,128)} %bitcast.19, f32[2,147456]{1,0:T(2,128)S(1)} %copy-done, f32[2]{0:T(128)S(1)} %rsqrt_reduce_fusion), kind=kLoop, calls=%fused_computation | loop fusion | flops 1179648 | bytes 3538952 | tf_op jit(solution)/shard_map/add | solution.py:463
  63.2 0.0 copy-done.1
  63.2 1.0 %copy.17 = f32[2,147456]{1,0:T(2,128)} copy(f32[2,147456]{1,0:T(2,128)S(1)} %bitcast.18) | data formatting | bytes 2359296
Async XLA Ops:
  0.6 59.5 %copy-start = (f32[2,147456]{1,0:T(2,128)S(1)}, f32[2,147456]{1,0:T(2,128)}, u32[]{:S(2)}) copy-start(f32[2,147456]{1,0:T(2,128)} %param.11) | copy-start | bytes 3538948
  60.1 3.1 %copy-start.1 = (f32[2304,128]{1,0:T(8,128)S(1)}, f32[2304,128]{1,0:T(8,128)}, u32[]{:S(2)}) copy-start(f32[2304,128]{1,0:T(8,128)} %get-tuple-element.5) | copy-start | bytes 3538948

commit v4 on v3

--- a/solution.py
+++ b/solution.py
@@ -39,9 +39,9 @@
 def step_kernel(
     cfg,
     feat_hbm, cot_hbm, ker_hbm, mom_hbm, w_in_hbm, b_in_hbm, w_out_hbm, b_out_hbm,
-    grads_flat, upd_flat, sq_out,
+    mom_flat, upd_flat,
     feat, cot, ker, mom_in, ker_in, w_in, b_in, w_out, b_out, load_sem,
-    edge, ns, we, cr, x3, y3, hid, pg, g, rc, s, rb, sq, grads_out, upd_out,
+    mom_all, sq_out, edge, ns, we, cr, x3, y3, hid, pg, g, rc, s, rb, sq, grads_out, upd_out,
     halo_send, halo_recv, core_send, core_recv, rs_send, rs_recv, sq_send, sq_recv,
     ag_send, ag_recv, fw_send, fw_recv,
 ):
@@ -65,7 +65,7 @@
         pltpu.make_async_copy(src, dst, load_sem.at[i])
         for i, (src, dst) in enumerate((
             (feat_hbm, feat), (cot_hbm, cot), (ker_hbm, ker), (w_in_hbm, w_in),
-            (b_in_hbm, b_in), (w_out_hbm, w_out), (b_out_hbm, b_out),
+            (b_in_hbm, b_in), (w_out_hbm, w_out), (b_out_hbm, b_out), (mom_hbm, mom_all),
         ))
     ]
     for part in parts:
@@ -75,10 +75,10 @@
         at = pl.multiple_of(part * true + at, TILE)
         twice = pl.multiple_of(2 * at, 2 * TILE)
         loads.append(pltpu.make_async_copy(
-            mom_hbm.at[pl.ds(twice, 2 * chunk)], mom_in.at[part], load_sem.at[7 + part]
+            mom_hbm.at[pl.ds(twice, 2 * chunk)], mom_in.at[part], load_sem.at[8 + part]
         ))
         loads.append(pltpu.make_async_copy(
-            ker_hbm.at[core, pl.ds(at, chunk)], ker_in.at[part], load_sem.at[10 + part]
+            ker_hbm.at[core, pl.ds(at, chunk)], ker_in.at[part], load_sem.at[11 + part]
         ))
     for copy in loads:
         copy.start()
@@ -323,6 +323,10 @@
     lax.fori_loop(1, owners, sq_start, 0)
 
     launch(0)
+    for part in parts:
+        collect(0, part)
+        if steps > 1:
+            spread(0, part, steps - 2)
 
     def sq_wait(d, tot):
         sq_copy(d).wait_recv()
@@ -364,20 +368,31 @@
     sent.append(sq_final)
 
     for step in reversed(range(steps)):
-        for k in range(2):
-            for part in parts:
-                collect(k, part)
-                if step > 0:
-                    spread(k, part, step - 1)
-    for k, flat in enumerate((grads_flat, upd_flat)):
-        for c in landing[k]:
-            c.wait_recv()
-        for layer in range(2):
-            for part in parts:
-                flat[pl.ds(2 * part * true + layer, true, stride=2), :] = outs[k][
-                    layer, pl.ds(base[part], true)
-                ]
+        for part in parts:
+            if step >= 1:
+                collect(0, part)
+            if step >= 2:
+                spread(0, part, step - 2)
+        for part in parts:
+            collect(1, part)
+            if step >= 1:
+                spread(1, part, step - 1)
     sq_final.wait_recv()
+    for c in landing[0]:
+        c.wait_recv()
+    for layer in range(2):
+        layer_norm = 1.0 / jnp.sqrt(sq_out[layer, 0:1] / param_count + 1e-06)
+        for part in parts:
+            at = pl.ds(2 * part * true + layer, true, stride=2)
+            mom_flat[at, :] = 0.9 * mom_all[at, :] + 0.1 * (
+                grads_out[layer, pl.ds(base[part], true)] * layer_norm
+            )
+    for c in landing[1]:
+        c.wait_recv()
+    for layer in range(2):
+        for part in parts:
+            at = pl.ds(2 * part * true + layer, true, stride=2)
+            upd_flat[at, :] = upd_out[layer, pl.ds(base[part], true)]
     for c in sent:
         c.wait_send()
 
@@ -405,15 +420,14 @@
     hidden_units = mlp_in_bias.shape[0]
     dma = pltpu.SemaphoreType.DMA
     full = (length, ch)
-    grads, update, squares = pl.pallas_call(
+    moved, update = pl.pallas_call(
         functools.partial(step_kernel, cfg),
         out_shape=(
             jax.ShapeDtypeStruct((18 * ch, ch), F32),
             jax.ShapeDtypeStruct((18 * ch, ch), F32),
-            jax.ShapeDtypeStruct((2, TILE, ch), F32),
         ),
         in_specs=[hbm] * 8,
-        out_specs=(vmem,) * 3,
+        out_specs=(vmem,) * 2,
         scratch_shapes=[
             pltpu.VMEM(features.shape, BF16),
             pltpu.VMEM(cotangent.shape, BF16),
@@ -424,7 +438,9 @@
             pltpu.SMEM((hidden_units,), F32),
             pltpu.SMEM((2, hidden_units), F32),
             pltpu.SMEM((2,), F32),
-            dma((13,)),
+            dma((14,)),
+            pltpu.VMEM((18 * ch, ch), F32),
+            pltpu.VMEM((2, TILE, ch), F32),
             pltpu.VMEM((2, 2, tile_rows, ch), BF16),
             pltpu.VMEM((2, 2, tile_cols, ch), BF16),
             pltpu.VMEM((2, 2, tile_rows, ch), BF16),
@@ -459,9 +475,7 @@
     def flat(values):
         return values.reshape(9 * ch, 2, ch).transpose(1, 0, 2).reshape(2, param_count)
 
-    norm = 1.0 / jnp.sqrt(squares[:, 0, :1] / float(param_count) + 1e-06)
-    momentum_out = 0.9 * momentum + 0.1 * (flat(grads) * norm)
-    return flat(update), momentum_out
+    return flat(update), flat(moved)
 
 
 def solution(mesh):

time: 64.4 us -> 65.9 us (1.023)
  other arithmetic: 3.89 us -> 0 us
  Pallas kernels: 58.6 us -> 61.8 us
  local copies, waits for them, and re-layouts: 1.02 us -> 3.23 us
    pallas_call x1, Pallas kernels: 58.6 us -> 61.8 us  [on_device(): pl.pallas_call(functools.partial(step_kernel, cfg), out_shape=(jax.ShapeD...]
    add x1 -> x0, other arithmetic: 3.09 us -> none  [on_device(): momentum_out = 0.9 * momentum + 0.1 * (flat(grads) * norm)]
    unnamed x5 -> x4, local copies, waits for them, and re-layouts: 1.02 us -> 3.23 us
    sqrt x1 -> x0, other arithmetic: 0.8 us -> none  [on_device(): norm = 1.0 / jnp.sqrt(squares[:, 0, :1] / float(param_count) + 1e-06)]
where the time goes in v4:
time: 65.9 us; the launch traced here: 65.7 us
  Pallas kernels  61.8 us (94%)
  local copies, waits for them, and re-layouts  3.23 us (5%)
    pallas_call x1, Pallas kernels, on_device(): pl.pallas_call(functools.partial(step_kernel, cfg), out_shape=(jax.ShapeD...  61.8 us
    unnamed x4, local copies, waits for them, and re-layouts  3.23 us

profile of v4, /device:TPU:1, one launch (start us, length us, event | category | flops | bytes accessed | tf_op | source)
XLA Modules:
  0.0 65.7 jit_solution(1843591579603069042)
XLA Ops:
  0.6 61.8 %shard_map.95 = (f32[2304,128]{1,0:T(8,128)}, f32[2304,128]{1,0:T(8,128)}) custom-call(bf16[64,32,128]{2,1,0:T(8,128)(2,1)} %feat_hbm.1, bf16[64,32,128]{2,1,0:T(8,128)(2,1)} %cot_hbm.1, bf16[2,1152,128]{2,1,0:T(8,128)(2,1)} %bitcast.20, f32[2304,128]{1,0:T(8,128)} %bitcast.17, f32[3,32]{1,0:T(4,128)} %bitcast.21, f32[32]{0:T(128)} %b_in_hbm.1, ...), custom_call_target="tpu_custom_call" | custom-call | tf_op jit(solution)/shard_map/pallas_call | solution.py:423
  62.5 0.0 copy-start
  62.5 2.2 %copy.15 = f32[2,147456]{1,0:T(2,128)} copy(f32[2,147456]{1,0:T(2,128)} %bitcast.19) | data formatting | bytes 2359296
  64.7 0.0 copy-done
  64.7 1.0 %copy.16 = f32[2,147456]{1,0:T(2,128)} copy(f32[2,147456]{1,0:T(2,128)S(1)} %bitcast.18) | data formatting | bytes 2359296
Async XLA Ops:
  62.5 2.2 %copy-start = (f32[2304,128]{1,0:T(8,128)S(1)}, f32[2304,128]{1,0:T(8,128)}, u32[]{:S(2)}) copy-start(f32[2304,128]{1,0:T(8,128)} %get-tuple-element.5) | copy-start | bytes 3538948
